TPU v7x, 32 devices: a whole 2x2x4 slice. The times are simulated.
32 devices in a mesh: expert: 8 (over z, x), hidden: 4 (over y, core).
Axes of the slice: x: 2, y: 2, z: 4, core: 2. Of those that a mesh axis runs over, the one named last changes fastest.
Arguments:
- tokens: bfloat16 [2, 16384, 512], P(None, ('expert', 'hidden')), may hold values from -6 to 6
- grad_out: bfloat16 [2, 16384, 512], P(None, ('expert', 'hidden')), may hold values from -6 to 6
- attn_routes: int32 [2, 16384, 4], P(None, ('expert', 'hidden')), may hold values from 0 to 23, all different within a row
- ffn_routes: int32 [2, 16384, 2], P(None, ('expert', 'hidden')), may hold values from 0 to 15, all different within a row; in each aligned block of 512 rows (0 to 511, 512 to 1023, ..., all dimensions but the last counted through in order) at most 128 rows name the same one
- segments: int32 [2, 64, 256], P(None, ('expert', 'hidden')), may hold values from 0 to 3, never falling along the last dimension, each value on 1 to 128 neighbouring positions
- pad_mask: int32 [2, 16384], P(None, ('expert', 'hidden')), may hold values 0 or 1
- norm1_gain: float32 [512], replicated, may hold values from 0.5 to 1.5
- norm1_bias: float32 [512], replicated, may hold values from -0.6 to 0.6
- attn_router: bfloat16 [512, 24], replicated, may hold values from -0.125 to 0.125
- query_w: bfloat16 [512, 1536], replicated, may hold values from -0.25 to 0.25
- key_w: bfloat16 [512, 64], replicated, may hold values from -0.25 to 0.25
- value_w: bfloat16 [512, 64], replicated, may hold values from -0.25 to 0.25
- attn_proj: bfloat16 [1536, 512], replicated, may hold values from -2 to 2
- norm2_gain: float32 [512], replicated, may hold values from 0.5 to 1.5
- norm2_bias: float32 [512], replicated, may hold values from -0.6 to 0.6
- ffn_router: bfloat16 [512, 16], replicated, may hold values from -0.1875 to 0.1875
- expert_in: bfloat16 [16, 512, 2048], P('expert', None, 'hidden'), may hold values from -0.25 to 0.25
- expert_out: bfloat16 [16, 2048, 512], P('expert', 'hidden'), may hold values from -0.1875 to 0.1875
- halt_w: float32 [512], replicated, may hold values from -0.25 to 0.25
- halt_b: float32 [1], replicated, may hold values from -2.5 to 2.5
Outputs:
- result: bfloat16 [2, 16384, 512], P(None, ('expert', 'hidden'))
- grad_tokens: float32 [2, 16384, 512], P(None, ('expert', 'hidden'))
- grad_norm1_gain: float32 [512], replicated
- grad_norm1_bias: float32 [512], replicated
- grad_attn_router: float32 [512, 24], replicated
- grad_query_w: float32 [512, 1536], replicated
- grad_key_w: float32 [512, 64], replicated
- grad_value_w: float32 [512, 64], replicated
- grad_attn_proj: float32 [1536, 512], replicated
- grad_norm2_gain: float32 [512], replicated
- grad_norm2_bias: float32 [512], replicated
- grad_ffn_router: float32 [512, 16], replicated
- grad_expert_in: float32 [16, 512, 2048], P('expert', None, 'hidden')
- grad_expert_out: float32 [16, 2048, 512], P('expert', 'hidden')
- grad_halt_w: float32 [512], replicated
- grad_halt_b: float32 [1], replicated
Inputs may be any that keep to these rules, and one draw needn't show every extreme that they name: `attn_routes`: each token names 4 different attention experts. `ffn_routes`: each token names 2 different feed-forward experts; in each micro-batch the 512 tokens of one device name no expert more than 128 times, a bound that some block reaches. `segments`: along a packed row the numbers never fall, and each of the 4 numbers covers 1 to 128 positions.
All inputs are finite; a program needn't handle non-finite values. No bound on the sum of `pad_mask` on one device may be relied on, other than what follows from the above.
Results may differ from a plain program's by a relative error of at most 0.015.
The roundings to bfloat16 on the way count: a program that leaves them out, or rounds other values in their place, can miss the bound.
Values may be sent and summed in bfloat16 or wider, within the bound.
A program may use at most 256 MiB of HBM per device.

v0:
```python
import jax
import jax.numpy as jnp
from jax import lax
from jax.sharding import PartitionSpec as P

SEQ = 256
ATT_BLOCK = 512


def layer_norm(value, gain, shift):
    center = value - jnp.mean(value, axis=-1, keepdims=True)
    spread = jnp.mean(center * center, axis=-1, keepdims=True)
    return center * lax.rsqrt(spread + 1e-05) * gain + shift


def norm_back(value, gain, shift, grad):
    unused, pullback = jax.vjp(layer_norm, value, gain, shift)
    return pullback(grad)


def gelu_back(pre, grad):
    unused, pullback = jax.vjp(jax.nn.gelu, pre)
    return pullback(grad)[0]


def softmax_back(probs, grad):
    return probs * (grad - jnp.sum(probs * grad, axis=-1, keepdims=True))


def spread_picks(pick, values):
    total = pick[:, 0, :, None] * values[:, 0, None, :]
    for which in range(1, pick.shape[1]):
        total = total + pick[:, which, :, None] * values[:, which, None, :]
    return total


def masked_scores(query_sel, keys, segment, padding):
    place = jnp.arange(segment.shape[0])
    same_row = place[:, None] // SEQ == place[None, :] // SEQ
    same_pair = segment[:, None] == segment[None, :]
    visible = (padding[None, :] == 1) | (place[:, None] == place[None, :])
    allowed = same_row & same_pair & visible
    scale = keys.shape[1] ** (-0.5)
    scores = jnp.einsum("qkh,jh->qkj", query_sel, keys, preferred_element_type=jnp.float32) * scale
    return jnp.where(allowed[:, None, :], scores, -1e30)


def attend_forward(operands):
    query_sel, keys, values, segment, padding = operands
    scores = masked_scores(query_sel, keys, segment, padding)
    top = jnp.max(scores, axis=-1, keepdims=True)
    expo = jnp.exp(scores - top)
    total = jnp.sum(expo, axis=-1, keepdims=True)
    probs = (expo / total).astype(jnp.bfloat16)
    heads = jnp.einsum("qkj,jh->qkh", probs, values, preferred_element_type=jnp.float32)
    return (heads, top + jnp.log(total))


def attend_backward(operands):
    query_sel, keys, values, segment, padding, logsum, grad_heads = operands
    scale = keys.shape[1] ** (-0.5)
    probs = jnp.exp(masked_scores(query_sel, keys, segment, padding) - logsum)
    probs_low = probs.astype(jnp.bfloat16)
    grad_values = jnp.einsum(
        "qkj,qkh->jh", probs_low, grad_heads, preferred_element_type=jnp.float32
    )
    grad_probs = jnp.einsum("qkh,jh->qkj", grad_heads, values, preferred_element_type=jnp.float32)
    grad_scores = softmax_back(probs, grad_probs).astype(jnp.bfloat16)
    grad_query = (
        jnp.einsum("qkj,jh->qkh", grad_scores, keys, preferred_element_type=jnp.float32) * scale
    )
    grad_keys = (
        jnp.einsum("qkj,qkh->jh", grad_scores, query_sel, preferred_element_type=jnp.float32)
        * scale
    )
    return (grad_query, grad_keys, grad_values)


def expert_forward(rows, first, second):
    pre = jnp.einsum("erd,edf->erf", rows, first, preferred_element_type=jnp.float32)
    act = jax.nn.gelu(pre).astype(jnp.bfloat16)
    total = jnp.einsum("erf,efd->erd", act, second, preferred_element_type=jnp.float32)
    return (pre, act, total)


def expert_backward(rows, pre, act, grad_rows_in, first, second):
    grad_act = jnp.einsum("erd,efd->erf", grad_rows_in, second, preferred_element_type=jnp.float32)
    grad_pre = gelu_back(pre, grad_act).astype(jnp.bfloat16)
    grad_second = jnp.einsum("erf,erd->efd", act, grad_rows_in, preferred_element_type=jnp.float32)
    grad_first = jnp.einsum("erd,erf->edf", rows, grad_pre, preferred_element_type=jnp.float32)
    grad_rows_out = jnp.einsum("erf,edf->erd", grad_pre, first, preferred_element_type=jnp.float32)
    return (grad_first, grad_second, grad_rows_out)


def per_device(
    tokens,
    grad_out,
    attn_routes,
    ffn_routes,
    segments,
    pad_mask,
    norm1_gain,
    norm1_bias,
    attn_router,
    query_w,
    key_w,
    value_w,
    attn_proj,
    norm2_gain,
    norm2_bias,
    ffn_router,
    expert_in,
    expert_out,
    halt_w,
    halt_b,
):
    micro_count, tok_rows, width = tokens.shape
    att_count = attn_router.shape[1]
    head = key_w.shape[1]
    experts_all = ffn_router.shape[1]
    top_ffn = ffn_routes.shape[2]
    capacity = 4 * tok_rows // experts_all
    blocks = tok_rows // ATT_BLOCK
    f32 = jnp.float32
    bf16 = jnp.bfloat16
    full_in, full_out = (
        lax.all_gather(expert_in, "hidden", axis=2, tiled=True),
        lax.all_gather(expert_out, "hidden", axis=1, tiled=True),
    )
    acc_in = jnp.zeros(full_in.shape, f32)
    acc_out = jnp.zeros(full_out.shape, f32)
    totals = (
        jnp.zeros(norm1_gain.shape, f32),
        jnp.zeros(norm1_bias.shape, f32),
        jnp.zeros(attn_router.shape, f32),
        jnp.zeros(query_w.shape, f32),
        jnp.zeros(key_w.shape, f32),
        jnp.zeros(value_w.shape, f32),
        jnp.zeros(attn_proj.shape, f32),
        jnp.zeros(norm2_gain.shape, f32),
        jnp.zeros(norm2_bias.shape, f32),
        jnp.zeros(ffn_router.shape, f32),
        jnp.zeros(halt_w.shape, f32),
        jnp.zeros(halt_b.shape, f32),
    )
    results = []
    grads_in = []
    for micro in range(micro_count):
        state_in = tokens[micro].astype(f32)
        segment = segments[micro].reshape(-1)
        padding = pad_mask[micro]
        route_attn = attn_routes[micro]
        route_ffn = ffn_routes[micro]
        normed = layer_norm(state_in, norm1_gain, norm1_bias)
        normed_low = normed.astype(bf16)
        logits_attn = jnp.dot(normed_low, attn_router, preferred_element_type=f32)
        pick_attn = (route_attn[:, :, None] == jnp.arange(att_count)[None, None, :]).astype(f32)
        gate_attn = jax.nn.softmax(jnp.sum(pick_attn * logits_attn[:, None, :], axis=-1), axis=-1)
        query_all = (
            jnp.dot(normed_low, query_w, preferred_element_type=f32)
            .astype(bf16)
            .reshape(tok_rows, att_count, head)
        )
        keys_low = jnp.dot(normed_low, key_w, preferred_element_type=f32).astype(bf16)
        values_low = jnp.dot(normed_low, value_w, preferred_element_type=f32).astype(bf16)
        pick_low = pick_attn.astype(bf16)
        query_sel = jnp.einsum(
            "tke,teh->tkh", pick_low, query_all, preferred_element_type=f32
        ).astype(bf16)
        block_query = query_sel.reshape(blocks, ATT_BLOCK, -1, head)
        block_keys = keys_low.reshape(blocks, ATT_BLOCK, head)
        block_values = values_low.reshape(blocks, ATT_BLOCK, head)
        block_segment = segment.reshape(blocks, ATT_BLOCK)
        block_padding = padding.reshape(blocks, ATT_BLOCK)
        heads, logsum = lax.map(
            attend_forward, (block_query, block_keys, block_values, block_segment, block_padding)
        )
        heads = heads.reshape(tok_rows, -1, head)
        mixed = spread_picks(pick_attn, gate_attn[:, :, None] * heads)
        mixed_low = mixed.reshape(tok_rows, -1).astype(bf16)
        state_mid = state_in + jnp.dot(mixed_low, attn_proj, preferred_element_type=f32)
        normed_two = layer_norm(state_mid, norm2_gain, norm2_bias)
        ffn_low = normed_two.astype(bf16)
        logits_ffn = jnp.dot(ffn_low, ffn_router, preferred_element_type=f32)
        pick_ffn = (route_ffn[:, :, None] == jnp.arange(experts_all)[None, None, :]).astype(f32)
        gate_ffn = jax.nn.softmax(jnp.sum(pick_ffn * logits_ffn[:, None, :], axis=-1), axis=-1)
        flat_route = route_ffn.reshape(-1)
        onehot = (flat_route[:, None] == jnp.arange(experts_all)[None, :]).astype(jnp.int32)
        rank = jnp.sum((jnp.cumsum(onehot, axis=0) - 1) * onehot, axis=1)
        slot = flat_route * capacity + rank
        outgoing = (
            jnp.zeros((experts_all * capacity, width), bf16)
            .at[slot]
            .set(jnp.repeat(ffn_low, top_ffn, axis=0))
        )
        arrived = lax.all_to_all(
            outgoing.reshape(experts_all, capacity, width),
            "expert",
            split_axis=0,
            concat_axis=1,
            tiled=True,
        )
        pre, act, expert_res = expert_forward(arrived, full_in, full_out)
        outgoing_back = expert_res.astype(bf16)
        returned = lax.all_to_all(
            outgoing_back, "expert", split_axis=1, concat_axis=0, tiled=True
        ).reshape(experts_all * capacity, width)
        picked = returned[slot].reshape(tok_rows, top_ffn, width).astype(f32)
        state_end = state_mid + jnp.sum(gate_ffn[:, :, None] * picked, axis=1)
        halting = jax.nn.sigmoid(jnp.sum(state_end * halt_w, axis=-1, keepdims=True) + halt_b)
        branch = state_end - state_in
        results.append((state_in + halting * branch).astype(bf16))
        grad_res = grad_out[micro].astype(f32)
        grad_halt = jnp.sum(grad_res * branch, axis=-1, keepdims=True) * halting * (1.0 - halting)
        grad_end = halting * grad_res + grad_halt * halt_w
        grad_state = grad_res * (1.0 - halting)
        grad_gate_ffn = jnp.sum(picked * grad_end[:, None, :], axis=-1)
        send_grad = (gate_ffn[:, :, None] * grad_end[:, None, :]).astype(bf16).reshape(-1, width)
        grad_buffer = jnp.zeros((experts_all * capacity, width), bf16).at[slot].set(send_grad)
        grad_arrived = lax.all_to_all(
            grad_buffer.reshape(experts_all, capacity, width),
            "expert",
            split_axis=0,
            concat_axis=1,
            tiled=True,
        )
        grad_first, grad_second, grad_rows_out = expert_backward(
            arrived, pre, act, grad_arrived, full_in, full_out
        )
        back_rows = grad_rows_out.astype(bf16)
        acc_in = acc_in + grad_first
        acc_out = acc_out + grad_second
        grad_back = lax.all_to_all(
            back_rows, "expert", split_axis=1, concat_axis=0, tiled=True
        ).reshape(experts_all * capacity, width)
        grad_slots = grad_back[slot].reshape(tok_rows, top_ffn, width).astype(f32)
        grad_sel_ffn = softmax_back(gate_ffn, grad_gate_ffn)
        grad_logits_ffn = jnp.sum(pick_ffn * grad_sel_ffn[:, :, None], axis=1).astype(bf16)
        grad_router_ffn = jnp.dot(ffn_low.T, grad_logits_ffn, preferred_element_type=f32)
        grad_normed_two = jnp.sum(grad_slots, axis=1) + jnp.dot(
            grad_logits_ffn, ffn_router.T, preferred_element_type=f32
        )
        grad_mid_norm, grad_gain_two, grad_bias_two = norm_back(
            state_mid, norm2_gain, norm2_bias, grad_normed_two
        )
        grad_mid = grad_end + grad_mid_norm
        grad_state = grad_state + grad_mid
        grad_attn = grad_mid.astype(bf16)
        grad_proj = jnp.dot(mixed_low.T, grad_attn, preferred_element_type=f32)
        grad_mixed = (
            jnp.dot(grad_attn, attn_proj.T, preferred_element_type=f32)
            .astype(bf16)
            .reshape(tok_rows, att_count, head)
        )
        grad_sel = jnp.einsum("tke,teh->tkh", pick_low, grad_mixed, preferred_element_type=f32)
        grad_gate_attn = jnp.sum(heads * grad_sel, axis=-1)
        grad_heads = (gate_attn[:, :, None] * grad_sel).astype(bf16)
        grad_query, grad_keys, grad_values = lax.map(
            attend_backward,
            (
                block_query,
                block_keys,
                block_values,
                block_segment,
                block_padding,
                logsum,
                grad_heads.reshape(blocks, ATT_BLOCK, -1, head),
            ),
        )
        grad_query_all = (
            spread_picks(pick_attn, grad_query.reshape(tok_rows, -1, head))
            .reshape(tok_rows, -1)
            .astype(bf16)
        )
        grad_keys_low = grad_keys.reshape(tok_rows, head).astype(bf16)
        grad_values_low = grad_values.reshape(tok_rows, head).astype(bf16)
        grad_query_w = jnp.dot(normed_low.T, grad_query_all, preferred_element_type=f32)
        grad_key_w = jnp.dot(normed_low.T, grad_keys_low, preferred_element_type=f32)
        grad_value_w = jnp.dot(normed_low.T, grad_values_low, preferred_element_type=f32)
        grad_sel_attn = softmax_back(gate_attn, grad_gate_attn)
        grad_logits_attn = jnp.sum(pick_attn * grad_sel_attn[:, :, None], axis=1).astype(bf16)
        grad_router_attn = jnp.dot(normed_low.T, grad_logits_attn, preferred_element_type=f32)
        grad_normed = (
            jnp.dot(grad_query_all, query_w.T, preferred_element_type=f32)
            + jnp.dot(grad_keys_low, key_w.T, preferred_element_type=f32)
            + jnp.dot(grad_values_low, value_w.T, preferred_element_type=f32)
            + jnp.dot(grad_logits_attn, attn_router.T, preferred_element_type=f32)
        )
        grad_in_norm, grad_gain_one, grad_bias_one = norm_back(
            state_in, norm1_gain, norm1_bias, grad_normed
        )
        grads_in.append(grad_state + grad_in_norm)
        grad_halt_w = jnp.sum(grad_halt * state_end, axis=0)
        grad_halt_b = jnp.sum(grad_halt, axis=0)
        summed = lax.psum(
            (
                grad_gain_one,
                grad_bias_one,
                grad_router_attn,
                grad_query_w,
                grad_key_w,
                grad_value_w,
                grad_proj,
                grad_gain_two,
                grad_bias_two,
                grad_router_ffn,
                grad_halt_w,
                grad_halt_b,
            ),
            ("expert", "hidden"),
        )
        totals = tuple(jax.tree.map(jnp.add, totals, tuple(summed)))
    acc_in, acc_out = (
        lax.psum_scatter(
            acc_in.astype(jnp.bfloat16), "hidden", scatter_dimension=2, tiled=True
        ).astype(jnp.float32),
        lax.psum_scatter(
            acc_out.astype(jnp.bfloat16), "hidden", scatter_dimension=1, tiled=True
        ).astype(jnp.float32),
    )
    return (
        jnp.stack(results),
        jnp.stack(grads_in),
        totals[0],
        totals[1],
        totals[2],
        totals[3],
        totals[4],
        totals[5],
        totals[6],
        totals[7],
        totals[8],
        totals[9],
        acc_in,
        acc_out,
        totals[10],
        totals[11],
    )


def solution(mesh):
    in_specs = (
        P(None, ("expert", "hidden"), None),
        P(None, ("expert", "hidden"), None),
        P(None, ("expert", "hidden"), None),
        P(None, ("expert", "hidden"), None),
        P(None, ("expert", "hidden"), None),
        P(None, ("expert", "hidden")),
        P(),
        P(),
        P(),
        P(),
        P(),
        P(),
        P(),
        P(),
        P(),
        P(),
        P("expert", None, "hidden"),
        P("expert", "hidden", None),
        P(),
        P(),
    )
    out_specs = (
        P(None, ("expert", "hidden"), None),
        P(None, ("expert", "hidden"), None),
        P(),
        P(),
        P(),
        P(),
        P(),
        P(),
        P(),
        P(),
        P(),
        P(),
        P("expert", None, "hidden"),
        P("expert", "hidden", None),
        P(),
        P(),
    )
    return jax.shard_map(
        per_device, mesh=mesh, in_specs=in_specs, out_specs=out_specs, check_vma=False
    )
```

profile of v0, /device:TPU:0, one launch (start us, length us, event | category | flops | bytes accessed | tf_op | source)
XLA Modules:
  0.0 937.1 jit_solution(10444804443158342972)
XLA Ops:
  27.1 8.9 select_reduce_fusion.3
  38.8 8.9 select_reduce_fusion.2
  134.6 7.2 scatter_custom_fusion.1
  141.8 7.4 all-to-all-start.2
  160.8 7.2 scatter_custom_fusion
  168.0 29.6 %all-to-all-done.2 = bf16[16,128,512]{2,1,0:T(8,128)(2,1)} async-done(((bf16[16,128,512]{2,1,0:T(8,128)(2,1)}), bf16[16,128,512]{2,1,0:T(8,128)(2,1)}, u32[]{:S(2)}, u32[]{:S(2)}) %all-to-all-start.2) | async-done | bytes 2097184 | tf_op jit(solution)/shard_map/all_to_all | solution.py:196
  205.4 13.1 %fusion.188 = f32[2,1024,2048]{2,1,0:T(8,128)} fusion(bf16[2,1024,512]{2,1,0:T(8,128)(2,1)} %bitcast.422, bf16[2,512,2048]{2,1,0:T(8,128)(2,1)} %all-gather.3.cloned.1.call-done), kind=kOutput, calls=%fused_computation.370 | convolution fusion | flops 4294967296 | bytes 23068672 | tf_op jit(solution)/shard_map/erd,edf->erf/dot_general | solution.py:80
  218.5 10.1 %convolution_convert_fusion.6 = bf16[2,1024,512]{2,1,0:T(8,128)(2,1)S(1)} fusion(bf16[2,2048,512]{2,1,0:T(8,128)(2,1)} %all-gather.5.cloned.1.call-done, f32[2,1024,2048]{2,1,0:T(8,128)} %fusion.188), kind=kOutput, calls=%fused_computation.71 | convolution fusion | flops 4333764608 | bytes 23068672 | tf_op jit(solution)/shard_map/erf,efd->erd/dot_general | solution.py:82
  232.1 18.0 %all-to-all-done = bf16[16,128,512]{2,1,0:T(8,128)(2,1)} async-done(((bf16[16,128,512]{2,1,0:T(8,128)(2,1)}), bf16[16,128,512]{2,1,0:T(8,128)(2,1)}, u32[]{:S(2)}, u32[]{:S(2)}) %all-to-all-start) | async-done | bytes 2097184 | tf_op jit(solution)/shard_map/all_to_all | solution.py:196
  257.5 10.4 %multiply_convert_fusion.1 = (bf16[2,1024,2048]{2,1,0:T(8,128)(2,1)S(1)}, f32[2,1024,2048]{2,1,0:T(8,128)}) fusion(bf16[2,1024,512]{2,1,0:T(8,128)(2,1)S(1)} %bitcast.424, bf16[2,512,2048]{2,1,0:T(8,128)(2,1)S(1)} %copy-done.202), kind=kOutput, calls=%fused_computation.27 | convolution fusion | flops 4332716032 | bytes 31457280 | tf_op jit(solution)/shard_map/erd,edf->erf/dot_general | solution.py:80
  276.1 26.4 %all-to-all-done.3 = bf16[2,1024,512]{2,0,1:T(2,128)(2,1)} async-done(((bf16[2,1024,512]{2,0,1:T(2,128)(2,1)}), bf16[2,1024,512]{2,0,1:T(2,128)(2,1)}, u32[]{:S(2)}, u32[]{:S(2)}) %all-to-all-start.3) | async-done | bytes 2097184 | tf_op jit(solution)/shard_map/all_to_all | solution.py:205
  321.6 7.0 gather_fusion.1
  339.8 15.0 %all-to-all-done.1 = bf16[2,1024,512]{2,0,1:T(2,128)(2,1)} async-done(((bf16[2,1024,512]{2,0,1:T(2,128)(2,1)}), bf16[2,1024,512]{2,0,1:T(2,128)(2,1)}, u32[]{:S(2)}, u32[]{:S(2)}) %all-to-all-start.1) | async-done | bytes 2097184 | tf_op jit(solution)/shard_map/all_to_all | solution.py:205
  358.2 7.0 gather_fusion
  389.2 8.2 scatter_custom_fusion.2
  411.0 7.7 scatter_custom_fusion.3
  418.8 30.8 %all-to-all-done.4 = bf16[16,128,512]{2,1,0:T(8,128)(2,1)} async-done(((bf16[16,128,512]{2,1,0:T(8,128)(2,1)}), bf16[16,128,512]{2,1,0:T(8,128)(2,1)}, u32[]{:S(2)}, u32[]{:S(2)}) %all-to-all-start.4) | async-done | bytes 2097184 | tf_op jit(solution)/shard_map/all_to_all | solution.py:220
  466.9 12.2 %fusion.194 = f32[2,2048,512]{2,1,0:T(8,128)} fusion(bf16[2,1024,2048]{2,1,0:T(8,128)(2,1)} %copy-done.208, bf16[2,1024,512]{2,1,0:T(8,128)(2,1)S(1)} %bitcast.426), kind=kOutput, calls=%fused_computation.376 | convolution fusion | flops 4294967296 | bytes 18874368 | tf_op jit(solution)/shard_map/erf,erd->efd/dot_general | solution.py:89
  479.1 22.7 %all-to-all-done.6 = bf16[16,128,512]{2,1,0:T(8,128)(2,1)} async-done(((bf16[16,128,512]{2,1,0:T(8,128)(2,1)}), bf16[16,128,512]{2,1,0:T(8,128)(2,1)}, u32[]{:S(2)}, u32[]{:S(2)}) %all-to-all-start.6) | async-done | bytes 2097184 | tf_op jit(solution)/shard_map/all_to_all | solution.py:220
  504.9 13.1 %add_convert_fusion = bf16[2,2048,512]{2,1,0:T(8,128)(2,1)} fusion(f32[2,2048,512]{2,1,0:T(8,128)} %fusion.194, bf16[2,1024,512]{2,1,0:T(8,128)(2,1)S(1)} %bitcast.428, f32[2,1024,2048]{2,1,0:T(8,128)} %fusion.188), kind=kOutput, calls=%fused_computation.28 | convolution fusion | flops 4336910336 | bytes 31457280 | tf_op jit(solution)/shard_map/erf,erd->efd/dot_general | solution.py:89
  518.0 20.5 %fusion.13 = bf16[2,1024,2048]{2,1,0:T(8,128)(2,1)} fusion(f32[2,1024,2048]{2,1,0:T(8,128)} %fusion.188, bf16[2,1024,512]{2,1,0:T(8,128)(2,1)} %bitcast.429, bf16[2,2048,512]{2,1,0:T(8,128)(2,1)} %all-gather.5.cloned.1.call-done), kind=kOutput, calls=%fused_computation.25 | convolution fusion | flops 4378853376 | bytes 31457280 | tf_op jit(solution)/shard_map/erd,efd->erf/dot_general | solution.py:87
  538.5 8.5 convolution_convert_fusion.4
  555.3 19.9 %fusion.6 = bf16[2,1024,2048]{2,1,0:T(8,128)(2,1)} fusion(f32[2,1024,2048]{2,1,0:T(8,128)} %get-tuple-element.359, bf16[2,1024,512]{2,1,0:T(8,128)(2,1)} %bitcast.427, bf16[2,2048,512]{2,1,0:T(8,128)(2,1)} %all-gather.5.cloned.1.call-done), kind=kOutput, calls=%fused_computation.18 | convolution fusion | flops 4378853376 | bytes 31457280 | tf_op jit(solution)/shard_map/erd,efd->erf/dot_general | solution.py:87
  575.2 8.5 convolution_convert_fusion.5
  587.2 15.7 %all-to-all-done.7 = bf16[2,1024,512]{2,0,1:T(2,128)(2,1)} async-done(((bf16[2,1024,512]{2,0,1:T(2,128)(2,1)}), bf16[2,1024,512]{2,0,1:T(2,128)(2,1)}, u32[]{:S(2)}, u32[]{:S(2)}) %all-to-all-start.7) | async-done | bytes 2097184 | tf_op jit(solution)/shard_map/all_to_all | solution.py:233
  609.6 7.9 fusion.193
  617.5 9.8 %add_convert_fusion.1 = bf16[2,512,2048]{2,1,0:T(8,128)(2,1)} fusion(f32[2,512,2048]{2,1,0:T(8,128)S(1)} %fusion.193, bf16[2,1024,512]{2,1,0:T(8,128)(2,1)S(1)} %bitcast.423, bf16[2,1024,2048]{2,1,0:T(8,128)(2,1)} %fusion.13), kind=kOutput, calls=%fused_computation.29 | convolution fusion | flops 4299161600 | bytes 23068672 | tf_op jit(solution)/shard_map/erd,erf->edf/dot_general | solution.py:90
  630.7 5.8 gather_fusion.3
  636.6 18.5 %all-to-all-done.5 = bf16[2,1024,512]{2,0,1:T(2,128)(2,1)} async-done(((bf16[2,1024,512]{2,0,1:T(2,128)(2,1)}), bf16[2,1024,512]{2,0,1:T(2,128)(2,1)}, u32[]{:S(2)}, u32[]{:S(2)}) %all-to-all-start.5) | async-done | bytes 2097184 | tf_op jit(solution)/shard_map/all_to_all | solution.py:233
  658.4 7.0 gather_fusion.2
  785.4 40.2 %all-reduce.6 = (f32[512]{0:T(512)}, f32[512]{0:T(512)}, f32[512,24]{0,1:T(8,128)}, f32[512]{0:T(512)}, f32[512]{0:T(512)}, /*index=5*/f32[512,16]{0,1:T(8,128)}, f32[512]{0:T(512)}, f32[1]{0:T(128)}) all-reduce(f32[512]{0:T(512)S(1)} %add.604, f32[512]{0:T(512)S(1)} %add.605, ...), channel_id=1, replica_groups=mesh['expert'=8,'hidden'=4] {'expert','hidden'}, use_global_device_ids=true, to_apply=%region_65.66 | all-reduce | flops 23041 | bytes 184328 | tf_op jit(solution)/shard_map/psum | solution.py:295
  831.4 92.1 %all-reduce.5.cloned.1.call-done = (f32[512,1536]{1,0:T(8,128)}, f32[512,64]{0,1:T(8,128)}, f32[512,64]{0,1:T(8,128)}, f32[1536,512]{1,0:T(8,128)}) async-done(((f32[512,1536]{1,0:T(8,128)}, f32[512,64]{0,1:T(8,128)}, f32[512,64]{0,1:T(8,128)}, f32[1536,512]{1,0:T(8,128)}), (f32[512,1536]{1,0:T(8,128)}, f32[512,64]{0,1:T(8,128)}, f32[512,64]{0,1:T(8,128)}, ...) | async-done | bytes 6553616 | tf_op jit(solution)/shard_map/psum | solution.py:295
  (706 shorter events, 393.1 us)
Async XLA Ops:
  7.2 111.5 %copy-start = (bf16[1536,512]{1,0:T(8,128)(2,1)S(1)}, bf16[1536,512]{1,0:T(8,128)(2,1)}, u32[]{:S(2)}) copy-start(bf16[1536,512]{1,0:T(8,128)(2,1)} %param.32) | copy-start | bytes 4718596
  7.2 198.2 %all-gather.3.cloned.1.call-start = ((), (), s32[]{:S(2)}) async-start(), calls=%async_computation.10 | async-start | bytes 5242880 | tf_op jit(solution)/shard_map/all_gather | solution.py:127
  7.9 210.6 %all-gather.5.cloned.1.call-start = ((), (), s32[]{:S(2)}) async-start(), calls=%async_computation.11 | async-start | bytes 5242880 | tf_op jit(solution)/shard_map/all_gather | solution.py:128
  13.8 441.7 %copy-start.5 = (bf16[1,512,512]{1,2,0:T(8,128)(2,1)}, bf16[1,512,512]{1,2,0:T(8,128)(2,1)S(1)}, u32[]{:S(2)}) copy-start(bf16[1,512,512]{1,2,0:T(8,128)(2,1)S(1)} %copy.704) | copy-start | bytes 1572868
  14.3 365.7 %copy-start.7 = (bf16[1,512,512]{1,2,0:T(8,128)(2,1)}, bf16[1,512,512]{1,2,0:T(8,128)(2,1)S(1)}, u32[]{:S(2)}) copy-start(bf16[1,512,512]{1,2,0:T(8,128)(2,1)S(1)} %copy.705) | copy-start | bytes 1572868
  15.7 38.6 %copy-start.14 = (bf16[512,512]{0,1:T(8,128)(2,1)}, bf16[512,512]{0,1:T(8,128)(2,1)S(1)}, u32[]{:S(2)}) copy-start(bf16[512,512]{0,1:T(8,128)(2,1)S(1)} %get-tuple-element.333) | copy-start | bytes 1572868
  15.9 104.8 %copy-start.73 = (bf16[512,64,1]{0,1,2:T(8,128)(2,1)}, bf16[512,64,1]{0,1,2:T(8,128)(2,1)S(1)}, u32[]{:S(2)}) copy-start(bf16[512,64,1]{0,1,2:T(8,128)(2,1)S(1)} %fusion.62) | copy-start | bytes 196612
  17.0 97.3 %copy-start.75 = (bf16[512,64,1]{0,1,2:T(8,128)(2,1)}, bf16[512,64,1]{0,1,2:T(8,128)(2,1)S(1)}, u32[]{:S(2)}) copy-start(bf16[512,64,1]{0,1,2:T(8,128)(2,1)S(1)} %fusion.64) | copy-start | bytes 196612
  20.1 75.2 %copy-start.44 = (s32[512,4]{1,0:T(8,128)}, s32[512,4]{1,0:T(8,128)S(1)}, u32[]{:S(2)}) copy-start(s32[512,4]{1,0:T(8,128)S(1)} %copy.585) | copy-start | bytes 24580
  37.1 47.5 %copy-start.105 = (f32[512,4]{0,1:T(4,128)}, f32[512,4]{0,1:T(4,128)S(1)}, u32[]{:S(2)}) copy-start(f32[512,4]{0,1:T(4,128)S(1)} %copy.588) | copy-start | bytes 24580
  50.4 36.7 %copy-start.103 = (f32[512,4]{0,1:T(4,128)}, f32[512,4]{0,1:T(4,128)S(1)}, u32[]{:S(2)}) copy-start(f32[512,4]{0,1:T(4,128)S(1)} %copy.611) | copy-start | bytes 24580
  87.8 27.9 %copy-start.122 = (f32[512,4]{0,1:T(4,128)}, f32[512,4]{0,1:T(4,128)S(1)}, u32[]{:S(2)}) copy-start(f32[512,4]{0,1:T(4,128)S(1)} %fusion.156) | copy-start | bytes 24580
  141.8 55.7 %all-to-all-start.2 = ((bf16[16,128,512]{2,1,0:T(8,128)(2,1)}), bf16[16,128,512]{2,1,0:T(8,128)(2,1)}, u32[]{:S(2)}, u32[]{:S(2)}) async-start(bf16[16,128,512]{2,1,0:T(8,128)(2,1)} %bitcast.410), calls=%async_computation.2 | async-start | bytes 4194304 | tf_op jit(solution)/shard_map/all_to_all | solution.py:196
  197.6 52.6 %all-to-all-start = ((bf16[16,128,512]{2,1,0:T(8,128)(2,1)}), bf16[16,128,512]{2,1,0:T(8,128)(2,1)}, u32[]{:S(2)}, u32[]{:S(2)}) async-start(bf16[16,128,512]{2,1,0:T(8,128)(2,1)} %bitcast.411), calls=%async_computation | async-start | bytes 4194304 | tf_op jit(solution)/shard_map/all_to_all | solution.py:196
  250.1 52.3 %all-to-all-start.3 = ((bf16[2,1024,512]{2,0,1:T(2,128)(2,1)}), bf16[2,1024,512]{2,0,1:T(2,128)(2,1)}, u32[]{:S(2)}, u32[]{:S(2)}) async-start(bf16[2,1024,512]{2,0,1:T(2,128)(2,1)} %copy.627), calls=%async_computation.3 | async-start | bytes 4194304 | tf_op jit(solution)/shard_map/all_to_all | solution.py:205
  302.5 52.4 %all-to-all-start.1 = ((bf16[2,1024,512]{2,0,1:T(2,128)(2,1)}), bf16[2,1024,512]{2,0,1:T(2,128)(2,1)}, u32[]{:S(2)}, u32[]{:S(2)}) async-start(bf16[2,1024,512]{2,0,1:T(2,128)(2,1)} %copy.604), calls=%async_computation.1 | async-start | bytes 4194304 | tf_op jit(solution)/shard_map/all_to_all | solution.py:205
  311.2 68.9 %copy-start.18 = (bf16[1,512,512]{1,2,0:T(8,128)(2,1)}, bf16[1,512,512]{1,2,0:T(8,128)(2,1)S(1)}, u32[]{:S(2)}) copy-start(bf16[1,512,512]{1,2,0:T(8,128)(2,1)S(1)} %copy.706) | copy-start | bytes 1572868
  318.2 39.9 %copy-start.140 = (s32[1024]{0:T(1024)}, s32[1024]{0:T(1024)S(1)}, u32[]{:S(2)}) copy-start(s32[1024]{0:T(1024)S(1)} %broadcast_clamp_fusion.1) | copy-start | bytes 12292
  397.3 52.3 %all-to-all-start.4 = ((bf16[16,128,512]{2,1,0:T(8,128)(2,1)}), bf16[16,128,512]{2,1,0:T(8,128)(2,1)}, u32[]{:S(2)}, u32[]{:S(2)}) async-start(bf16[16,128,512]{2,1,0:T(8,128)(2,1)} %bitcast.409), calls=%async_computation.4 | async-start | bytes 4194304 | tf_op jit(solution)/shard_map/all_to_all | solution.py:220
  402.6 289.6 %copy-start.135 = (f32[512]{0:T(512)}, f32[512]{0:T(512)S(1)}, u32[]{:S(2)}) copy-start(f32[512]{0:T(512)S(1)} %get-tuple-element.276) | copy-start | bytes 6148
  418.8 36.7 %copy-start.113 = (f32[512]{0:T(512)S(1)}, f32[512]{0:T(512)}, u32[]{:S(2)}) copy-start(f32[512]{0:T(512)} %param.26) | copy-start | bytes 6148
  418.8 36.7 %copy-start.116 = (f32[512]{0:T(512)S(1)}, f32[512]{0:T(512)}, u32[]{:S(2)}) copy-start(f32[512]{0:T(512)} %copy-done.115) | copy-start | bytes 6148
  418.8 36.7 %copy-start.133 = (f32[512]{0:T(512)S(1)}, f32[512]{0:T(512)}, u32[]{:S(2)}) copy-start(f32[512]{0:T(512)} %copy-done.132) | copy-start | bytes 6148
  418.8 36.7 %copy-start.177 = (f32[512]{0:T(512)S(1)}, f32[512]{0:T(512)}, u32[]{:S(2)}) copy-start(f32[512]{0:T(512)} %param.27) | copy-start | bytes 6148
  418.8 37.7 %copy-start.27 = (f32[512,512]{1,0:T(8,128)S(1)}, f32[512,512]{1,0:T(8,128)}, u32[]{:S(2)}) copy-start(f32[512,512]{1,0:T(8,128)} %copy-done.26) | copy-start | bytes 3145732
  449.6 52.2 %all-to-all-start.6 = ((bf16[16,128,512]{2,1,0:T(8,128)(2,1)}), bf16[16,128,512]{2,1,0:T(8,128)(2,1)}, u32[]{:S(2)}, u32[]{:S(2)}) async-start(bf16[16,128,512]{2,1,0:T(8,128)(2,1)} %bitcast.408), calls=%async_computation.6 | async-start | bytes 4194304 | tf_op jit(solution)/shard_map/all_to_all | solution.py:220
  454.0 371.6 %reduce-scatter.5.cloned.1.call-start = ((), (), s32[]{:S(2)}) async-start(), calls=%async_computation.13 | async-start | bytes 5242880 | tf_op jit(solution)/shard_map/reduce_scatter | solution.py:317
  550.5 52.4 %all-to-all-start.7 = ((bf16[2,1024,512]{2,0,1:T(2,128)(2,1)}), bf16[2,1024,512]{2,0,1:T(2,128)(2,1)}, u32[]{:S(2)}, u32[]{:S(2)}) async-start(bf16[2,1024,512]{2,0,1:T(2,128)(2,1)} %copy.656), calls=%async_computation.7 | async-start | bytes 4194304 | tf_op jit(solution)/shard_map/all_to_all | solution.py:233
  602.9 52.2 %all-to-all-start.5 = ((bf16[2,1024,512]{2,0,1:T(2,128)(2,1)}), bf16[2,1024,512]{2,0,1:T(2,128)(2,1)}, u32[]{:S(2)}, u32[]{:S(2)}) async-start(bf16[2,1024,512]{2,0,1:T(2,128)(2,1)} %copy.634), calls=%async_computation.5 | async-start | bytes 4194304 | tf_op jit(solution)/shard_map/all_to_all | solution.py:233
  607.3 221.2 %reduce-scatter.3.cloned.1.call-start = ((), (), s32[]{:S(2)}) async-start(), calls=%async_computation.12 | async-start | bytes 5242880 | tf_op jit(solution)/shard_map/reduce_scatter | solution.py:314
  627.3 296.2 %all-reduce.5.cloned.1.call-start = ((), (), s32[]{:S(2)}) async-start(), calls=%async_computation.14 | async-start | bytes 13107200 | tf_op jit(solution)/shard_map/psum | solution.py:295
  636.6 21.8 %copy-start.141 = (s32[1024]{0:T(1024)S(1)}, s32[1024]{0:T(1024)}, u32[]{:S(2)}) copy-start(s32[1024]{0:T(1024)} %copy-done.140) | copy-start | bytes 12292
  (190 other events, 921.7 us)
Sparse Core Ops, SparseCore 0:
  9.6 37.1 all-gather.2
  48.4 34.5 all-gather.4
  518.1 43.5 reduce-scatter.4
  627.4 45.7 reduce-scatter.2
  764.6 158.8 all-reduce.4
where the time goes:
time: 944 us; the launch traced here: 937 us
  waiting for transfers between devices  270 us (29%)
  local copies, waits for them, and re-layouts  224 us (24%)
  matrix products  212 us (22%)
  other arithmetic  133 us (14%)
  blocking collectives  40.2 us (4%)
  starting transfers between devices  39.6 us (4%)
  between operations  18.8 us (2%)
    psum x1, waiting for transfers between devices, per_device(): lax.psum((grad_gain_one, grad_bias_one, grad_router_attn, grad_query_w, g...  92.1 us
    all_to_all x2, waiting for transfers between devices, per_device(): lax.all_to_all(grad_buffer.reshape(experts_all, capacity, width), 'expert...  53.6 us
    all_to_all x2, waiting for transfers between devices, per_device(): lax.all_to_all(outgoing.reshape(experts_all, capacity, width), 'expert',...  47.6 us
    all_to_all x2, waiting for transfers between devices, per_device(): lax.all_to_all(outgoing_back, 'expert', split_axis=1, concat_axis=0, tile...  41.4 us
    dot_general x2, matrix products, expert_backward(): jnp.einsum('erd,efd->erf', grad_rows_in, second, preferred_element_type=j...  40.4 us
    psum x1, blocking collectives, per_device(): lax.psum((grad_gain_one, grad_bias_one, grad_router_attn, grad_query_w, g...  40.2 us
    all_to_all x2, waiting for transfers between devices, per_device(): lax.all_to_all(back_rows, 'expert', split_axis=1, concat_axis=0, tiled=True)  34.2 us
    unnamed x431, local copies, waits for them, and re-layouts  27 us
  transfers between devices with their start and end apart: 13, of which 9 were waited for; matrix products, arithmetic and copies ran while one was open for 53% of the time, Pallas kernels for 0%

commit v1 on v0

--- a/solution.py
+++ b/solution.py
@@ -293,21 +293,24 @@
         grad_halt_w = jnp.sum(grad_halt * state_end, axis=0)
         grad_halt_b = jnp.sum(grad_halt, axis=0)
         summed = lax.psum(
-            (
-                grad_gain_one,
-                grad_bias_one,
-                grad_router_attn,
-                grad_query_w,
-                grad_key_w,
-                grad_value_w,
-                grad_proj,
-                grad_gain_two,
-                grad_bias_two,
-                grad_router_ffn,
-                grad_halt_w,
-                grad_halt_b,
+            lax.psum(
+                (
+                    grad_gain_one,
+                    grad_bias_one,
+                    grad_router_attn,
+                    grad_query_w,
+                    grad_key_w,
+                    grad_value_w,
+                    grad_proj,
+                    grad_gain_two,
+                    grad_bias_two,
+                    grad_router_ffn,
+                    grad_halt_w,
+                    grad_halt_b,
+                ),
+                "hidden",
             ),
-            ("expert", "hidden"),
+            "expert",
         )
         totals = tuple(jax.tree.map(jnp.add, totals, tuple(summed)))
     acc_in, acc_out = (

time: 944 us -> 1210 us (1.28)
  waiting for transfers between devices: 270 us -> 515 us
  blocking collectives: 40.2 us -> 53.5 us
    psum x0 -> x1, waiting for transfers between devices: none -> 224 us  [per_device(): lax.psum(lax.psum((grad_gain_one, grad_bias_one, grad_router_attn, grad_q...]
    psum x0 -> x1, blocking collectives: none -> 38.5 us  [per_device(): lax.psum(lax.psum((grad_gain_one, grad_bias_one, grad_router_attn, grad_q...]
    psum x1, blocking collectives: 40.2 us -> 15 us  [per_device(): lax.psum((grad_gain_one, grad_bias_one, grad_router_attn, grad_query_w, g...]
    all_to_all x2, waiting for transfers between devices: 53.6 us -> 75.5 us  [per_device(): lax.all_to_all(grad_buffer.reshape(experts_all, capacity, width), 'expert...]
    psum x1, waiting for transfers between devices: 92.1 us -> 71.7 us  [per_device(): lax.psum((grad_gain_one, grad_bias_one, grad_router_attn, grad_query_w, g...]
    all_to_all x2, waiting for transfers between devices: 34.2 us -> 46.7 us  [per_device(): lax.all_to_all(back_rows, 'expert', split_axis=1, concat_axis=0, tiled=True)]
    unnamed x431 -> x425, local copies, waits for them, and re-layouts: 27 us -> 26.9 us
  transfers between devices with their start and end apart: 13 -> 14, of which waited for: 9 -> 11; matrix products, arithmetic and copies ran while one was open for 53% -> 32% of each run, Pallas kernels for 0% -> 0%
where the time goes in v1:
time: 1210 us; the launch traced here: 1200 us
  waiting for transfers between devices  515 us (43%)
  local copies, waits for them, and re-layouts  226 us (19%)
  matrix products  216 us (18%)
  other arithmetic  132 us (11%)
  blocking collectives  53.5 us (4%)
  starting transfers between devices  40 us (3%)
  between operations  19.1 us (2%)
    psum x1, waiting for transfers between devices, per_device(): lax.psum(lax.psum((grad_gain_one, grad_bias_one, grad_router_attn, grad_q...  224 us
    all_to_all x2, waiting for transfers between devices, per_device(): lax.all_to_all(grad_buffer.reshape(experts_all, capacity, width), 'expert...  75.5 us
    psum x1, waiting for transfers between devices, per_device(): lax.psum((grad_gain_one, grad_bias_one, grad_router_attn, grad_query_w, g...  71.7 us
    all_to_all x2, waiting for transfers between devices, per_device(): lax.all_to_all(outgoing.reshape(experts_all, capacity, width), 'expert',...  47.6 us
    all_to_all x2, waiting for transfers between devices, per_device(): lax.all_to_all(back_rows, 'expert', split_axis=1, concat_axis=0, tiled=True)  46.7 us
    all_to_all x2, waiting for transfers between devices, per_device(): lax.all_to_all(outgoing_back, 'expert', split_axis=1, concat_axis=0, tile...  41.4 us
    psum x1, blocking collectives, per_device(): lax.psum(lax.psum((grad_gain_one, grad_bias_one, grad_router_attn, grad_q...  38.5 us
    dot_general x2, matrix products, expert_backward(): jnp.einsum('erd,efd->erf', grad_rows_in, second, preferred_element_type=j...  36.8 us
  transfers between devices with their start and end apart: 14, of which 11 were waited for; matrix products, arithmetic and copies ran while one was open for 32% of the time, Pallas kernels for 0%

profile of v1, /device:TPU:0, one launch (start us, length us, event | category | flops | bytes accessed | tf_op | source)
XLA Modules:
  0.0 1201.1 jit_solution(11296982589351600339)
XLA Ops:
  26.7 8.9 select_reduce_fusion.3
  38.3 8.9 select_reduce_fusion.2
  133.6 7.2 scatter_custom_fusion.1
  140.8 7.4 all-to-all-start.2
  159.8 7.2 scatter_custom_fusion
  167.0 29.6 %all-to-all-done.2 = bf16[16,128,512]{2,1,0:T(8,128)(2,1)} async-done(((bf16[16,128,512]{2,1,0:T(8,128)(2,1)}), bf16[16,128,512]{2,1,0:T(8,128)(2,1)}, u32[]{:S(2)}, u32[]{:S(2)}) %all-to-all-start.2) | async-done | bytes 2097184 | tf_op jit(solution)/shard_map/all_to_all | solution.py:196
  204.2 13.1 %fusion.188 = f32[2,1024,2048]{2,1,0:T(8,128)} fusion(bf16[2,1024,512]{2,1,0:T(8,128)(2,1)} %bitcast.422, bf16[2,512,2048]{2,1,0:T(8,128)(2,1)} %all-gather.3.cloned.1.call-done), kind=kOutput, calls=%fused_computation.370 | convolution fusion | flops 4294967296 | bytes 23068672 | tf_op jit(solution)/shard_map/erd,edf->erf/dot_general | solution.py:80
  217.3 10.1 convolution_convert_fusion.6
  230.9 18.0 %all-to-all-done = bf16[16,128,512]{2,1,0:T(8,128)(2,1)} async-done(((bf16[16,128,512]{2,1,0:T(8,128)(2,1)}), bf16[16,128,512]{2,1,0:T(8,128)(2,1)}, u32[]{:S(2)}, u32[]{:S(2)}) %all-to-all-start) | async-done | bytes 2097184 | tf_op jit(solution)/shard_map/all_to_all | solution.py:196
  256.3 10.4 multiply_convert_fusion.1
  274.9 26.4 %all-to-all-done.3 = bf16[2,1024,512]{2,0,1:T(2,128)(2,1)} async-done(((bf16[2,1024,512]{2,0,1:T(2,128)(2,1)}), bf16[2,1024,512]{2,0,1:T(2,128)(2,1)}, u32[]{:S(2)}, u32[]{:S(2)}) %all-to-all-start.3) | async-done | bytes 2097184 | tf_op jit(solution)/shard_map/all_to_all | solution.py:205
  320.5 7.0 gather_fusion.1
  338.7 15.0 %all-to-all-done.1 = bf16[2,1024,512]{2,0,1:T(2,128)(2,1)} async-done(((bf16[2,1024,512]{2,0,1:T(2,128)(2,1)}), bf16[2,1024,512]{2,0,1:T(2,128)(2,1)}, u32[]{:S(2)}, u32[]{:S(2)}) %all-to-all-start.1) | async-done | bytes 2097184 | tf_op jit(solution)/shard_map/all_to_all | solution.py:205
  357.0 7.0 gather_fusion
  388.0 8.2 scatter_custom_fusion.2
  409.9 7.7 scatter_custom_fusion.3
  417.7 30.9 %all-to-all-done.4 = bf16[16,128,512]{2,1,0:T(8,128)(2,1)} async-done(((bf16[16,128,512]{2,1,0:T(8,128)(2,1)}), bf16[16,128,512]{2,1,0:T(8,128)(2,1)}, u32[]{:S(2)}, u32[]{:S(2)}) %all-to-all-start.4) | async-done | bytes 2097184 | tf_op jit(solution)/shard_map/all_to_all | solution.py:220
  456.2 44.6 %all-to-all-done.6 = bf16[16,128,512]{2,1,0:T(8,128)(2,1)} async-done(((bf16[16,128,512]{2,1,0:T(8,128)(2,1)}), bf16[16,128,512]{2,1,0:T(8,128)(2,1)}, u32[]{:S(2)}, u32[]{:S(2)}) %all-to-all-start.6) | async-done | bytes 2097184 | tf_op jit(solution)/shard_map/all_to_all | solution.py:220
  503.7 17.0 %fusion.13 = bf16[2,1024,2048]{2,1,0:T(8,128)(2,1)} fusion(f32[2,1024,2048]{2,1,0:T(8,128)} %fusion.188, bf16[2,1024,512]{2,1,0:T(8,128)(2,1)S(1)} %bitcast.428, bf16[2,2048,512]{2,1,0:T(8,128)(2,1)S(1)} %copy-done.202), kind=kOutput, calls=%fused_computation.25 | convolution fusion | flops 4378853376 | bytes 31457280 | tf_op jit(solution)/shard_map/erd,efd->erf/dot_general | solution.py:87
  520.7 9.1 convolution_convert_fusion.4
  537.9 19.8 %fusion.6 = bf16[2,1024,2048]{2,1,0:T(8,128)(2,1)} fusion(f32[2,1024,2048]{2,1,0:T(8,128)} %get-tuple-element.371, bf16[2,1024,512]{2,1,0:T(8,128)(2,1)} %bitcast.426, bf16[2,2048,512]{2,1,0:T(8,128)(2,1)} %all-gather.5.cloned.1.call-done), kind=kOutput, calls=%fused_computation.18 | convolution fusion | flops 4378853376 | bytes 31457280 | tf_op jit(solution)/shard_map/erd,efd->erf/dot_general | solution.py:87
  557.7 8.5 convolution_convert_fusion.5
  569.7 15.9 %all-to-all-done.7 = bf16[2,1024,512]{2,0,1:T(2,128)(2,1)} async-done(((bf16[2,1024,512]{2,0,1:T(2,128)(2,1)}), bf16[2,1024,512]{2,0,1:T(2,128)(2,1)}, u32[]{:S(2)}, u32[]{:S(2)}) %all-to-all-start.7) | async-done | bytes 2097184 | tf_op jit(solution)/shard_map/all_to_all | solution.py:233
  607.0 30.8 %all-to-all-done.5 = bf16[2,1024,512]{2,0,1:T(2,128)(2,1)} async-done(((bf16[2,1024,512]{2,0,1:T(2,128)(2,1)}), bf16[2,1024,512]{2,0,1:T(2,128)(2,1)}, u32[]{:S(2)}, u32[]{:S(2)}) %all-to-all-start.5) | async-done | bytes 2097184 | tf_op jit(solution)/shard_map/all_to_all | solution.py:233
  741.4 11.9 fusion.194
  753.4 13.3 %add_convert_fusion = bf16[2,2048,512]{2,1,0:T(8,128)(2,1)} fusion(f32[2,2048,512]{2,1,0:T(8,128)} %fusion.194, bf16[2,1024,512]{2,1,0:T(8,128)(2,1)S(1)} %bitcast.429, f32[2,1024,2048]{2,1,0:T(8,128)} %fusion.188), kind=kOutput, calls=%fused_computation.28 | convolution fusion | flops 4336910336 | bytes 31457280 | tf_op jit(solution)/shard_map/erf,erd->efd/dot_general | solution.py:89
  766.8 7.9 fusion.193
  774.7 9.9 add_convert_fusion.1
  793.1 71.7 %all-reduce.11.cloned.1.call-done = (f32[512,1536]{1,0:T(8,128)}, f32[512,64]{0,1:T(8,128)}, f32[512,64]{0,1:T(8,128)}, f32[1536,512]{1,0:T(8,128)}) async-done(((f32[512,1536]{1,0:T(8,128)}, f32[512,64]{0,1:T(8,128)}, f32[512,64]{0,1:T(8,128)}, f32[1536,512]{1,0:T(8,128)}), (f32[512,1536]{1,0:T(8,128)}, f32[512,64]{0,1:T(8,128)}, f32[512,64]{0,1:T(8,128)}, ...) | async-done | bytes 6553616 | tf_op jit(solution)/shard_map/psum | solution.py:296
  897.6 15.0 %all-reduce.12 = (f32[512]{0:T(512)S(1)}, f32[512]{0:T(512)S(1)}, f32[512,24]{0,1:T(8,128)S(1)}, f32[512]{0:T(512)S(1)}, f32[512]{0:T(512)S(1)}, /*index=5*/f32[512,16]{0,1:T(8,128)S(1)}, f32[512]{0:T(512)S(1)}, f32[1]{0:T(128)}) all-reduce(f32[512]{0:T(512)S(1)} %add.652, ...), channel_id=1, replica_groups=mesh['expert'=8,'hidden'=4] {'hidden'}, use_global_device_ids=true, to_apply=%region_65.66 | all-reduce | flops 23041 | bytes 184328 | tf_op jit(solution)/shard_map/psum | solution.py:296
  912.5 38.5 %all-reduce.13 = (f32[512]{0:T(512)}, f32[512]{0:T(512)}, f32[512,24]{0,1:T(8,128)}, f32[512]{0:T(512)}, f32[512]{0:T(512)}, /*index=5*/f32[512,16]{0,1:T(8,128)}, f32[512]{0:T(512)}, f32[1]{0:T(128)}) all-reduce(f32[512]{0:T(512)S(1)} %get-tuple-element.274, ...), channel_id=1, replica_groups=mesh['expert'=8,'hidden'=4] {'expert'}, use_global_device_ids=true, to_apply=%region_66.67 | all-reduce | flops 23041 | bytes 184328 | tf_op jit(solution)/shard_map/psum | solution.py:295
  963.3 223.8 %all-reduce.9.cloned.1.call-done = (f32[512,1536]{1,0:T(8,128)}, f32[512,64]{0,1:T(8,128)}, f32[512,64]{0,1:T(8,128)}, f32[1536,512]{1,0:T(8,128)}) async-done(((f32[512,1536]{1,0:T(8,128)}, f32[512,64]{0,1:T(8,128)}, f32[512,64]{0,1:T(8,128)}, f32[1536,512]{1,0:T(8,128)}), (f32[512,1536]{1,0:T(8,128)}, f32[512,64]{0,1:T(8,128)}, f32[512,64]{0,1:T(8,128)}, ...) | async-done | bytes 6553616 | tf_op jit(solution)/shard_map/psum | solution.py:295
  (704 shorter events, 421.3 us)
Async XLA Ops:
  7.2 110.9 %copy-start = (bf16[1536,512]{1,0:T(8,128)(2,1)S(1)}, bf16[1536,512]{1,0:T(8,128)(2,1)}, u32[]{:S(2)}) copy-start(bf16[1536,512]{1,0:T(8,128)(2,1)} %param.32) | copy-start | bytes 4718596
  7.2 197.0 %all-gather.3.cloned.1.call-start = ((), (), s32[]{:S(2)}) async-start(), calls=%async_computation.10 | async-start | bytes 5242880 | tf_op jit(solution)/shard_map/all_gather | solution.py:127
  7.9 209.4 %all-gather.5.cloned.1.call-start = ((), (), s32[]{:S(2)}) async-start(), calls=%async_computation.11 | async-start | bytes 5242880 | tf_op jit(solution)/shard_map/all_gather | solution.py:128
  14.3 364.6 %copy-start.5 = (bf16[1,512,512]{1,2,0:T(8,128)(2,1)}, bf16[1,512,512]{1,2,0:T(8,128)(2,1)S(1)}, u32[]{:S(2)}) copy-start(bf16[1,512,512]{1,2,0:T(8,128)(2,1)S(1)} %copy.705) | copy-start | bytes 1572868
  15.6 38.3 %copy-start.13 = (bf16[512,512]{0,1:T(8,128)(2,1)}, bf16[512,512]{0,1:T(8,128)(2,1)S(1)}, u32[]{:S(2)}) copy-start(bf16[512,512]{0,1:T(8,128)(2,1)S(1)} %get-tuple-element.345) | copy-start | bytes 1572868
  15.8 103.6 %copy-start.68 = (bf16[512,64,1]{0,1,2:T(8,128)(2,1)}, bf16[512,64,1]{0,1,2:T(8,128)(2,1)S(1)}, u32[]{:S(2)}) copy-start(bf16[512,64,1]{0,1,2:T(8,128)(2,1)S(1)} %fusion.62) | copy-start | bytes 196612
  16.9 96.7 %copy-start.70 = (bf16[512,64,1]{0,1,2:T(8,128)(2,1)}, bf16[512,64,1]{0,1,2:T(8,128)(2,1)S(1)}, u32[]{:S(2)}) copy-start(bf16[512,64,1]{0,1,2:T(8,128)(2,1)S(1)} %fusion.64) | copy-start | bytes 196612
  20.0 74.6 %copy-start.42 = (s32[512,4]{1,0:T(8,128)}, s32[512,4]{1,0:T(8,128)S(1)}, u32[]{:S(2)}) copy-start(s32[512,4]{1,0:T(8,128)S(1)} %copy.585) | copy-start | bytes 24580
  36.6 47.2 %copy-start.103 = (f32[512,4]{0,1:T(4,128)}, f32[512,4]{0,1:T(4,128)S(1)}, u32[]{:S(2)}) copy-start(f32[512,4]{0,1:T(4,128)S(1)} %copy.588) | copy-start | bytes 24580
  50.0 36.4 %copy-start.101 = (f32[512,4]{0,1:T(4,128)}, f32[512,4]{0,1:T(4,128)S(1)}, u32[]{:S(2)}) copy-start(f32[512,4]{0,1:T(4,128)S(1)} %copy.611) | copy-start | bytes 24580
  87.1 28.0 %copy-start.125 = (f32[512,4]{0,1:T(4,128)}, f32[512,4]{0,1:T(4,128)S(1)}, u32[]{:S(2)}) copy-start(f32[512,4]{0,1:T(4,128)S(1)} %fusion.156) | copy-start | bytes 24580
  140.8 55.8 %all-to-all-start.2 = ((bf16[16,128,512]{2,1,0:T(8,128)(2,1)}), bf16[16,128,512]{2,1,0:T(8,128)(2,1)}, u32[]{:S(2)}, u32[]{:S(2)}) async-start(bf16[16,128,512]{2,1,0:T(8,128)(2,1)} %bitcast.410), calls=%async_computation.2 | async-start | bytes 4194304 | tf_op jit(solution)/shard_map/all_to_all | solution.py:196
  196.6 52.3 %all-to-all-start = ((bf16[16,128,512]{2,1,0:T(8,128)(2,1)}), bf16[16,128,512]{2,1,0:T(8,128)(2,1)}, u32[]{:S(2)}, u32[]{:S(2)}) async-start(bf16[16,128,512]{2,1,0:T(8,128)(2,1)} %bitcast.411), calls=%async_computation | async-start | bytes 4194304 | tf_op jit(solution)/shard_map/all_to_all | solution.py:196
  248.9 52.4 %all-to-all-start.3 = ((bf16[2,1024,512]{2,0,1:T(2,128)(2,1)}), bf16[2,1024,512]{2,0,1:T(2,128)(2,1)}, u32[]{:S(2)}, u32[]{:S(2)}) async-start(bf16[2,1024,512]{2,0,1:T(2,128)(2,1)} %copy.627), calls=%async_computation.3 | async-start | bytes 4194304 | tf_op jit(solution)/shard_map/all_to_all | solution.py:205
  301.3 52.4 %all-to-all-start.1 = ((bf16[2,1024,512]{2,0,1:T(2,128)(2,1)}), bf16[2,1024,512]{2,0,1:T(2,128)(2,1)}, u32[]{:S(2)}, u32[]{:S(2)}) async-start(bf16[2,1024,512]{2,0,1:T(2,128)(2,1)} %copy.604), calls=%async_computation.1 | async-start | bytes 4194304 | tf_op jit(solution)/shard_map/all_to_all | solution.py:205
  310.1 68.9 %copy-start.17 = (bf16[1,512,512]{1,2,0:T(8,128)(2,1)}, bf16[1,512,512]{1,2,0:T(8,128)(2,1)S(1)}, u32[]{:S(2)}) copy-start(bf16[1,512,512]{1,2,0:T(8,128)(2,1)S(1)} %copy.706) | copy-start | bytes 1572868
  378.9 295.9 %copy-start.134 = (f32[512]{0:T(512)}, f32[512]{0:T(512)S(1)}, u32[]{:S(2)}) copy-start(f32[512]{0:T(512)S(1)} %get-tuple-element.291) | copy-start | bytes 6148
  378.9 295.9 %copy-start.148 = (f32[512]{0:T(512)}, f32[512]{0:T(512)S(1)}, u32[]{:S(2)}) copy-start(f32[512]{0:T(512)S(1)} %get-tuple-element.290) | copy-start | bytes 6148
  396.2 52.3 %all-to-all-start.4 = ((bf16[16,128,512]{2,1,0:T(8,128)(2,1)}), bf16[16,128,512]{2,1,0:T(8,128)(2,1)}, u32[]{:S(2)}, u32[]{:S(2)}) async-start(bf16[16,128,512]{2,1,0:T(8,128)(2,1)} %bitcast.408), calls=%async_computation.4 | async-start | bytes 4194304 | tf_op jit(solution)/shard_map/all_to_all | solution.py:220
  401.5 273.4 %copy-start.140 = (f32[512]{0:T(512)}, f32[512]{0:T(512)S(1)}, u32[]{:S(2)}) copy-start(f32[512]{0:T(512)S(1)} %get-tuple-element.288) | copy-start | bytes 6148
  401.5 273.4 %copy-start.161 = (f32[512]{0:T(512)}, f32[512]{0:T(512)S(1)}, u32[]{:S(2)}) copy-start(f32[512]{0:T(512)S(1)} %get-tuple-element.287) | copy-start | bytes 6148
  448.5 52.3 %all-to-all-start.6 = ((bf16[16,128,512]{2,1,0:T(8,128)(2,1)}), bf16[16,128,512]{2,1,0:T(8,128)(2,1)}, u32[]{:S(2)}, u32[]{:S(2)}) async-start(bf16[16,128,512]{2,1,0:T(8,128)(2,1)} %bitcast.409), calls=%async_computation.6 | async-start | bytes 4194304 | tf_op jit(solution)/shard_map/all_to_all | solution.py:220
  533.3 52.4 %all-to-all-start.7 = ((bf16[2,1024,512]{2,0,1:T(2,128)(2,1)}), bf16[2,1024,512]{2,0,1:T(2,128)(2,1)}, u32[]{:S(2)}, u32[]{:S(2)}) async-start(bf16[2,1024,512]{2,0,1:T(2,128)(2,1)} %copy.656), calls=%async_computation.7 | async-start | bytes 4194304 | tf_op jit(solution)/shard_map/all_to_all | solution.py:233
  569.7 21.9 %copy-start.27 = (f32[512,512]{1,0:T(8,128)S(1)}, f32[512,512]{1,0:T(8,128)}, u32[]{:S(2)}) copy-start(f32[512,512]{1,0:T(8,128)} %copy-done.26) | copy-start | bytes 3145732
  585.7 52.2 %all-to-all-start.5 = ((bf16[2,1024,512]{2,0,1:T(2,128)(2,1)}), bf16[2,1024,512]{2,0,1:T(2,128)(2,1)}, u32[]{:S(2)}, u32[]{:S(2)}) async-start(bf16[2,1024,512]{2,0,1:T(2,128)(2,1)} %copy.634), calls=%async_computation.5 | async-start | bytes 4194304 | tf_op jit(solution)/shard_map/all_to_all | solution.py:233
  590.0 274.8 %all-reduce.11.cloned.1.call-start = ((), (), s32[]{:S(2)}) async-start(), calls=%async_computation.15 | async-start | bytes 13107200 | tf_op jit(solution)/shard_map/psum | solution.py:296
  597.7 73.0 %copy-start.105 = (bf16[512,16]{0,1:T(8,128)(2,1)}, bf16[512,16]{0,1:T(8,128)(2,1)S(1)}, u32[]{:S(2)}) copy-start(bf16[512,16]{0,1:T(8,128)(2,1)S(1)} %select_reduce_fusion.5) | copy-start | bytes 49156
  597.8 71.4 %copy-start.106 = (bf16[512,16]{0,1:T(8,128)(2,1)}, bf16[512,16]{0,1:T(8,128)(2,1)S(1)}, u32[]{:S(2)}) copy-start(bf16[512,16]{0,1:T(8,128)(2,1)S(1)} %select_reduce_fusion.4) | copy-start | bytes 49156
  741.2 209.8 %reduce-scatter.5.cloned.1.call-start = ((), (), s32[]{:S(2)}) async-start(), calls=%async_computation.13 | async-start | bytes 5242880 | tf_op jit(solution)/shard_map/reduce_scatter | solution.py:320
  766.8 193.7 %reduce-scatter.3.cloned.1.call-start = ((), (), s32[]{:S(2)}) async-start(), calls=%async_computation.12 | async-start | bytes 5242880 | tf_op jit(solution)/shard_map/reduce_scatter | solution.py:317
  784.6 402.5 %all-reduce.9.cloned.1.call-start = ((), (), s32[]{:S(2)}) async-start(), calls=%async_computation.14 | async-start | bytes 13107200 | tf_op jit(solution)/shard_map/psum | solution.py:295
  791.8 73.0 %copy-start.127 = (f32[512,4]{0,1:T(4,128)}, f32[512,4]{0,1:T(4,128)S(1)}, u32[]{:S(2)}) copy-start(f32[512,4]{0,1:T(4,128)S(1)} %multiply_reduce_fusion.17) | copy-start | bytes 24580
  (188 other events, 928.5 us)
Sparse Core Ops, SparseCore 0:
  9.6 37.2 all-gather.2
  48.4 34.4 all-gather.4
  741.3 123.3 all-reduce.10
  867.1 46.1 reduce-scatter.4
  915.9 44.5 reduce-scatter.2
  964.9 222.2 all-reduce.8
